TPU v7x, 128 devices: a whole 4x4x4 slice. The times are simulated.
128 devices in a mesh: rep: 4 (over x), shard: 32 (over z, y, core).
Axes of the slice: x: 4, y: 4, z: 4, core: 2. Of those that a mesh axis runs over, the one named last changes fastest.
Arguments:
- attention_grad: bfloat16 [4, 8, 768, 768], P('rep', None, 'shard'), may hold values from -45 to 45
- dense_grad: bfloat16 [4, 2, 3072, 768], P('rep', None, 'shard'), may hold values from -45 to 45
- embedding_grad: bfloat16 [4, 8192, 768], P('rep', 'shard'), may hold values from -45 to 45
- attention_error: float32 [4, 8, 768, 768], P('rep', None, 'shard'), may hold values from -4 to 4
- dense_error: float32 [4, 2, 3072, 768], P('rep', None, 'shard'), may hold values from -4 to 4
- embedding_error: float32 [4, 8192, 768], P('rep', 'shard'), may hold values from -4 to 4
- attention_weight: float32 [8, 768, 768], P(None, 'shard'), may hold values from -0.21875 to 0.21875
- dense_weight: float32 [2, 3072, 768], P(None, 'shard'), may hold values from -0.21875 to 0.21875
- embedding_weight: float32 [8192, 768], P('shard'), may hold values from -0.21875 to 0.21875
- attention_momentum: float32 [8, 768, 768], P(None, 'shard'), may hold values from -1.5 to 1.5
- dense_momentum: float32 [2, 3072, 768], P(None, 'shard'), may hold values from -1.5 to 1.5
- embedding_momentum: float32 [8192, 768], P('shard'), may hold values from -1.5 to 1.5
- warm_start: float32 [11, 32, 768], replicated, may hold values from -0.21875 to 0.21875
- norm_scale: float32 [3, 768], P(None, 'shard'), may hold values from 0.5 to 1.5
- norm_momentum: float32 [3, 768], P(None, 'shard'), may hold values from -1.5 to 1.5
- norm_grad: float32 [4, 3, 768], P('rep', None, 'shard'), may hold values from -6 to 6
Outputs:
- attention_updated: float32 [8, 768, 768], P(None, 'shard')
- dense_updated: float32 [2, 3072, 768], P(None, 'shard')
- embedding_updated: float32 [8192, 768], P('shard')
- attention_copy: bfloat16 [8, 768, 768], P(None, 'shard')
- dense_copy: bfloat16 [2, 3072, 768], P(None, 'shard')
- embedding_copy: bfloat16 [8192, 768], P('shard')
- attention_residue: float32 [4, 8, 768, 768], P('rep', None, 'shard')
- dense_residue: float32 [4, 2, 3072, 768], P('rep', None, 'shard')
- embedding_residue: float32 [4, 8192, 768], P('rep', 'shard')
- attention_velocity: float32 [8, 768, 768], P(None, 'shard')
- dense_velocity: float32 [2, 3072, 768], P(None, 'shard')
- embedding_velocity: float32 [8192, 768], P('shard')
- next_start: float32 [11, 32, 768], replicated
- norm_updated: float32 [3, 768], P(None, 'shard')
- norm_velocity: float32 [3, 768], P(None, 'shard')
All inputs are finite; a program needn't handle non-finite values.
Results may differ from a plain program's by a relative error of at most 0.001.
Values sent between devices are 32-bit elements; how exact they have to be, the bound alone decides.
A program may use at most 64 MiB of HBM per device.

v0:
```python
import jax
import jax.numpy as jnp
from jax import lax
from jax.sharding import PartitionSpec as P


def invert(grams):
    factor = jnp.linalg.cholesky(grams)
    identity = jnp.broadcast_to(jnp.eye(grams.shape[-1], dtype=grams.dtype), grams.shape)
    return lax.linalg.triangular_solve(factor, identity, left_side=True, lower=True)


def finish(merged, approx, weight, momentum):
    velocity = 0.9 * momentum + approx
    updated = weight - 0.05 * velocity
    return (updated, updated.astype(jnp.bfloat16), (merged - approx)[None], velocity)


def body(
    attention_grad,
    dense_grad,
    embedding_grad,
    attention_error,
    dense_error,
    embedding_error,
    attention_weight,
    dense_weight,
    embedding_weight,
    attention_momentum,
    dense_momentum,
    embedding_momentum,
    warm_start,
    norm_scale,
    norm_momentum,
    norm_grad,
):
    highest = lax.Precision.HIGHEST
    replicas = lax.axis_size("rep")
    norm_total = lax.psum(norm_grad[0], "rep")
    merged_attention = attention_grad[0].astype(jnp.float32) + attention_error[0]
    merged_dense = dense_grad[0].astype(jnp.float32) + dense_error[0]
    merged_embedding = embedding_grad[0].astype(jnp.float32) + embedding_error[0]
    proj_attention = jnp.einsum("mkc,mrc->mkr", warm_start[:8], merged_attention, precision=highest)
    proj_dense = jnp.einsum("mkc,mrc->mkr", warm_start[8:10], merged_dense, precision=highest)
    proj_embedding = jnp.einsum("kc,rc->kr", warm_start[10], merged_embedding, precision=highest)
    proj_attention, proj_dense, proj_embedding = lax.psum(
        (proj_attention, proj_dense, proj_embedding), "rep"
    )
    proj_attention = proj_attention / replicas
    proj_dense = proj_dense / replicas
    proj_embedding = proj_embedding / replicas
    local_grams = jnp.concatenate(
        [
            jnp.einsum("mkr,mjr->mkj", proj_attention, proj_attention, precision=highest),
            jnp.einsum("mkr,mjr->mkj", proj_dense, proj_dense, precision=highest),
            jnp.einsum("kr,jr->kj", proj_embedding, proj_embedding, precision=highest)[None],
        ],
        0,
    )
    grams = lax.psum(local_grams, "shard")
    inverse = invert(grams)
    ortho_attention = jnp.einsum("mjk,mkr->mjr", inverse[:8], proj_attention, precision=highest)
    ortho_dense = jnp.einsum("mjk,mkr->mjr", inverse[8:10], proj_dense, precision=highest)
    ortho_embedding = jnp.einsum("jk,kr->jr", inverse[10], proj_embedding, precision=highest)
    partial_right = jnp.concatenate(
        [
            jnp.einsum("mkr,mrc->mkc", ortho_attention, merged_attention, precision=highest),
            jnp.einsum("mkr,mrc->mkc", ortho_dense, merged_dense, precision=highest),
            jnp.einsum("kr,rc->kc", ortho_embedding, merged_embedding, precision=highest)[None],
        ],
        0,
    )
    next_start = lax.psum(partial_right, ("rep", "shard")) / replicas
    approx_attention = jnp.einsum(
        "mkr,mkc->mrc", ortho_attention, next_start[:8], precision=highest
    )
    approx_dense = jnp.einsum("mkr,mkc->mrc", ortho_dense, next_start[8:10], precision=highest)
    approx_embedding = jnp.einsum("kr,kc->rc", ortho_embedding, next_start[10], precision=highest)
    a_upd, a_copy, a_res, a_vel = finish(
        merged_attention, approx_attention, attention_weight, attention_momentum
    )
    d_upd, d_copy, d_res, d_vel = finish(merged_dense, approx_dense, dense_weight, dense_momentum)
    e_upd, e_copy, e_res, e_vel = finish(
        merged_embedding, approx_embedding, embedding_weight, embedding_momentum
    )
    norm_velocity = 0.9 * norm_momentum + norm_total / replicas
    norm_updated = norm_scale - 0.05 * norm_velocity
    return (
        a_upd,
        d_upd,
        e_upd,
        a_copy,
        d_copy,
        e_copy,
        a_res,
        d_res,
        e_res,
        a_vel,
        d_vel,
        e_vel,
        next_start,
        norm_updated,
        norm_velocity,
    )


def solution(mesh):
    return jax.shard_map(
        body,
        mesh=mesh,
        in_specs=(
            P("rep", None, "shard", None),
            P("rep", None, "shard", None),
            P("rep", "shard", None),
            P("rep", None, "shard", None),
            P("rep", None, "shard", None),
            P("rep", "shard", None),
            P(None, "shard", None),
            P(None, "shard", None),
            P("shard", None),
            P(None, "shard", None),
            P(None, "shard", None),
            P("shard", None),
            P(),
            P(None, "shard"),
            P(None, "shard"),
            P("rep", None, "shard"),
        ),
        out_specs=(
            P(None, "shard", None),
            P(None, "shard", None),
            P("shard", None),
            P(None, "shard", None),
            P(None, "shard", None),
            P("shard", None),
            P("rep", None, "shard", None),
            P("rep", None, "shard", None),
            P("rep", "shard", None),
            P(None, "shard", None),
            P(None, "shard", None),
            P("shard", None),
            P(),
            P(None, "shard"),
            P(None, "shard"),
        ),
        check_vma=False,
    )
```

profile of v0, /device:TPU:1, one launch (start us, length us, event | category | flops | bytes accessed | tf_op | source)
XLA Modules:
  0.0 417.3 jit_solution(11912199704461353907)
XLA Ops:
  7.2 0.0 copy-start.2
  7.2 0.0 copy-start.6
  7.2 0.0 all-reduce.6.cloned.1.call-start
  7.2 1.3 copy.47
  8.6 0.0 copy-start.1
  8.6 2.7 convolution_bitcast_fusion.2
  11.3 0.0 copy-done.2
  11.3 0.0 copy-done.6
  11.3 2.2 convolution_bitcast_fusion.3
  13.5 0.0 copy-done.1
  13.5 0.0 copy-done.5
  13.5 2.6 convolution_bitcast_fusion
  16.1 0.0 all-reduce.6.cloned.1.call-update
  16.1 0.0 all-reduce.4.cloned.1.call-start
  16.2 41.9 %all-reduce.6.cloned.1.call-done = (f32[32,256]{1,0:T(8,128)}, f32[2,32,96]{2,1,0:T(8,128)}, f32[8,32,24]{1,2,0:T(8,128)}, f32[3,24]{1,0:T(4,128)}) async-done(((f32[32,256]{1,0:T(8,128)}, f32[2,32,96]{2,1,0:T(8,128)}, f32[8,32,24]{1,2,0:T(8,128)}, f32[3,24]{1,0:T(4,128)}), (f32[32,256]{1,0:T(8,128)}, f32[2,32,96]{2,1,0:T(8,128)}, f32[8,32,24]{1,2,0:T(8,128)}, ...) | async-done | bytes 82224 | tf_op jit(solution)/shard_map/psum | solution.py:46
  58.2 1.0 convolution_bitcast_fusion.4
  59.2 1.0 fusion.35
  60.2 1.4 fusion.25
  61.6 0.0 copy-start.13
  61.6 125.0 %psum.45 = f32[11,32,32]{1,2,0:T(8,128)S(1)} all-reduce(f32[11,32,32]{1,2,0:T(8,128)S(1)} %pad_maximum_fusion.1), channel_id=1, replica_groups=mesh['rep'=4,'shard'=32] {'shard'}, use_global_device_ids=true, to_apply=%region_3.0 | all-reduce | flops 11264 | bytes 90112 | tf_op jit(solution)/shard_map/psum | solution.py:60
  186.6 0.1 copy.39
  186.7 0.0 copy-start
  186.7 0.0 copy-start.4
  186.7 0.7 fusion.19
  187.4 32.9 %custom-call.7 = f32[11,32,32]{2,1,0:T(8,128)S(1)} custom-call(f32[11,32,32]{2,1,0:T(8,128)} %fusion.19), custom_call_target="Cholesky" | custom-call | tf_op jit(solution)/shard_map/jit(cholesky)/cholesky | solution.py:8
  220.4 0.1 compare_reduce_fusion
  220.5 0.1 select_bitcast_fusion
  220.6 27.1 %custom-call.8 = f32[11,1,32,32]{2,3,1,0:T(8,128)S(1)} custom-call(f32[11,1,32,32]{3,2,1,0:T(8,128)S(1)} %select_bitcast_fusion), custom_call_target="InvertDiagBlocksLowerTriangular" | custom-call | tf_op jit(solution)/shard_map/triangular_solve | solution.py:10
  247.7 0.5 fusion.17
  248.2 0.0 copy-done.13
  248.2 0.3 fusion.23
  248.5 0.9 fusion.30
  249.5 0.9 fusion.33
  250.4 0.0 copy-done
  250.4 0.0 copy-done.4
  250.4 0.6 convolution_bitcast_fusion.1
  251.0 0.4 fusion.6
  251.5 0.8 fusion.10
  252.3 1.1 pad_maximum_fusion
  253.4 0.0 copy-start.14
  253.4 0.0 copy-start.15
  253.4 0.0 copy-start.16
  253.4 0.0 all-reduce.4.cloned.1.call-update
  253.4 0.7 copy-done.14
  254.1 0.0 copy-done.15
  254.1 0.0 copy-done.16
  254.1 0.6 multiply_subtract_fusion.3
  254.7 147.5 %all-reduce.4.cloned.1.call-done = f32[11,32,768]{2,1,0:T(8,128)} async-done(((f32[11,32,768]{2,1,0:T(8,128)}), f32[11,32,768]{2,1,0:T(8,128)}) %all-reduce.4.cloned.1.call-update) | async-done | bytes 1081360 | tf_op jit(solution)/shard_map/psum | solution.py:73
  402.2 0.0 copy-start.9
  402.2 0.0 copy-start.10
  402.2 1.4 broadcast_multiply_fusion
  403.6 0.0 copy-done.9
  403.6 0.1 copy-done.10
  403.7 0.0 copy-start.3
  403.7 0.0 copy-start.11
  403.7 2.1 fusion.50
  405.8 0.0 copy-done.11
  405.8 0.0 copy-done.12
  405.8 0.0 copy-start.8
  405.8 2.1 fusion.49
  407.9 0.0 copy-done.3
  407.9 0.0 copy-done.7
  407.9 0.0 copy-done.8
  407.9 2.5 fusion.48
  (8 shorter events, 0.1 us)
Async XLA Ops:
  7.2 4.1 copy-start.2
  7.2 4.1 copy-start.6
  7.2 51.0 %all-reduce.6.cloned.1.call-start = ((), (), s32[]{:S(2)}) async-start(), calls=%async_computation.1 | async-start | bytes 331776 | tf_op jit(solution)/shard_map/psum | solution.py:46
  8.6 4.9 %copy-start.1 = (f32[1,8,24,768]{3,2,1,0:T(8,128)S(1)}, f32[1,8,24,768]{3,2,1,0:T(8,128)}, u32[]{:S(2)}) copy-start(f32[1,8,24,768]{3,2,1,0:T(8,128)} %param.19) | copy-start | bytes 1769476
  8.6 4.9 %copy-start.5 = (bf16[1,8,24,768]{3,2,1,0:T(8,128)(2,1)S(1)}, bf16[1,8,24,768]{3,2,1,0:T(8,128)(2,1)}, u32[]{:S(2)}) copy-start(bf16[1,8,24,768]{3,2,1,0:T(8,128)(2,1)} %param.16) | copy-start | bytes 884740
  16.1 386.0 %all-reduce.4.cloned.1.call-start = ((), (), s32[]{:S(2)}) async-start(), calls=%async_computation | async-start | bytes 2162688 | tf_op jit(solution)/shard_map/psum | solution.py:73
  61.6 186.6 %copy-start.13 = (f32[8,32,24]{1,2,0:T(8,128)S(1)}, f32[8,32,24]{1,2,0:T(8,128)}, u32[]{:S(2)}) copy-start(f32[8,32,24]{1,2,0:T(8,128)} %get-tuple-element.17) | copy-start | bytes 73732
  186.7 63.7 %copy-start = (f32[1,256,768]{2,1,0:T(8,128)S(1)}, f32[1,256,768]{2,1,0:T(8,128)}, u32[]{:S(2)}) copy-start(f32[1,256,768]{2,1,0:T(8,128)} %param.21) | copy-start | bytes 2359300
  186.7 63.7 %copy-start.4 = (bf16[1,256,768]{2,1,0:T(8,128)(2,1)S(1)}, bf16[1,256,768]{2,1,0:T(8,128)(2,1)}, u32[]{:S(2)}) copy-start(bf16[1,256,768]{2,1,0:T(8,128)(2,1)} %param.18) | copy-start | bytes 1179652
  253.4 0.7 copy-start.14
  253.4 0.7 copy-start.15
  253.4 0.7 copy-start.16
  402.2 1.4 copy-start.9
  402.2 1.6 copy-start.10
  403.7 4.2 %copy-start.3 = (f32[11,32,768]{2,1,0:T(8,128)}, f32[11,32,768]{2,1,0:T(8,128)S(1)}, u32[]{:S(2)}) copy-start(f32[11,32,768]{2,1,0:T(8,128)S(1)} %broadcast_multiply_fusion) | copy-start | bytes 3244036
  403.7 2.1 copy-start.11
  403.7 2.1 copy-start.12
  405.8 2.1 copy-start.7
  405.8 2.1 copy-start.8
Sparse Core Ops, SparseCore 0:
  16.3 41.8 all-reduce.5
  253.5 148.5 all-reduce.3
where the time goes:
time: 418 us; the launch traced here: 417 us
  waiting for transfers between devices  189 us (45%)
  blocking collectives  125 us (30%)
  other arithmetic  64.1 us (15%)
  matrix products  22.1 us (5%)
  between operations  14.3 us (3%)
    psum x1, waiting for transfers between devices, body(): next_start = lax.psum(partial_right, ('rep', 'shard')) / replicas  147 us
    psum x1, blocking collectives, body(): grams = lax.psum(local_grams, 'shard')  125 us
    psum x1, waiting for transfers between devices, body(): lax.psum((proj_attention, proj_dense, proj_embedding), 'rep')  41.9 us
    another operation x4, other arithmetic, invert(): factor = jnp.linalg.cholesky(grams)  33.1 us
    another operation x3, other arithmetic, invert(): lax.linalg.triangular_solve(factor, identity, left_side=True, lower=True)  27.2 us
  transfers between devices with their start and end apart: 2, of which 2 were waited for; matrix products, arithmetic and copies ran while one was open for 0% of the time, Pallas kernels for 0%

commit v1 on v0

--- a/solution.py
+++ b/solution.py
@@ -70,7 +70,7 @@
         ],
         0,
     )
-    next_start = lax.psum(partial_right, ("rep", "shard")) / replicas
+    next_start = lax.psum(lax.psum(partial_right, "shard"), "rep") / replicas
     approx_attention = jnp.einsum(
         "mkr,mkc->mrc", ortho_attention, next_start[:8], precision=highest
     )

time: 418 us -> 422 us (level)
  waiting for transfers between devices: 189 us -> 194 us
    psum x1 -> x2, waiting for transfers between devices: 147 us -> 152 us  [body(): next_start = lax.psum(lax.psum(partial_right, 'shard'), 'rep') / replicas]
  transfers between devices with their start and end apart: 2 -> 3, of which waited for: 2 -> 3; matrix products, arithmetic and copies ran while one was open for 0% -> 0% of each run, Pallas kernels for 0% -> 0%
where the time goes in v1:
time: 422 us; the launch traced here: 421 us
  waiting for transfers between devices  194 us (46%)
  blocking collectives  125 us (30%)
  other arithmetic  64.1 us (15%)
  matrix products  22.1 us (5%)
  between operations  14 us (3%)
    psum x2, waiting for transfers between devices, body(): next_start = lax.psum(lax.psum(partial_right, 'shard'), 'rep') / replicas  152 us
    psum x1, blocking collectives, body(): grams = lax.psum(local_grams, 'shard')  125 us
    psum x1, waiting for transfers between devices, body(): lax.psum((proj_attention, proj_dense, proj_embedding), 'rep')  41.9 us
    another operation x4, other arithmetic, invert(): factor = jnp.linalg.cholesky(grams)  33.1 us
    another operation x3, other arithmetic, invert(): lax.linalg.triangular_solve(factor, identity, left_side=True, lower=True)  27.2 us
  transfers between devices with their start and end apart: 3, of which 3 were waited for; matrix products, arithmetic and copies ran while one was open for 0% of the time, Pallas kernels for 0%

profile of v1, /device:TPU:1, one launch (start us, length us, event | category | flops | bytes accessed | tf_op | source)
XLA Modules:
  0.0 421.1 jit_solution(1752593810938974026)
XLA Ops:
  7.2 0.0 copy-start.2
  7.2 0.0 copy-start.6
  7.2 0.0 all-reduce.9.cloned.1.call-start
  7.2 1.3 copy.47
  8.6 0.0 copy-start.1
  8.6 2.7 convolution_bitcast_fusion.2
  11.3 0.0 copy-done.2
  11.3 0.0 copy-done.6
  11.3 2.2 convolution_bitcast_fusion.3
  13.5 0.0 copy-done.1
  13.5 0.0 copy-done.5
  13.5 2.6 convolution_bitcast_fusion
  16.1 0.0 all-reduce.9.cloned.1.call-update
  16.1 0.0 all-reduce.5.cloned.1.call-start
  16.2 41.9 %all-reduce.9.cloned.1.call-done = (f32[32,256]{1,0:T(8,128)}, f32[2,32,96]{2,1,0:T(8,128)}, f32[8,32,24]{1,2,0:T(8,128)}, f32[3,24]{1,0:T(4,128)}) async-done(((f32[32,256]{1,0:T(8,128)}, f32[2,32,96]{2,1,0:T(8,128)}, f32[8,32,24]{1,2,0:T(8,128)}, f32[3,24]{1,0:T(4,128)}), (f32[32,256]{1,0:T(8,128)}, f32[2,32,96]{2,1,0:T(8,128)}, f32[8,32,24]{1,2,0:T(8,128)}, ...) | async-done | bytes 82224 | tf_op jit(solution)/shard_map/psum | solution.py:46
  58.2 1.0 convolution_bitcast_fusion.4
  59.2 1.0 fusion.35
  60.2 1.4 fusion.25
  61.6 0.0 copy-start.13
  61.6 125.0 %psum.52 = f32[11,32,32]{1,2,0:T(8,128)S(1)} all-reduce(f32[11,32,32]{1,2,0:T(8,128)S(1)} %pad_maximum_fusion.1), channel_id=1, replica_groups=mesh['rep'=4,'shard'=32] {'shard'}, use_global_device_ids=true, to_apply=%region_3.0 | all-reduce | flops 11264 | bytes 90112 | tf_op jit(solution)/shard_map/psum | solution.py:60
  186.6 0.1 copy.39
  186.7 0.0 copy-start
  186.7 0.0 copy-start.4
  186.7 0.7 fusion.19
  187.4 32.9 %custom-call.7 = f32[11,32,32]{2,1,0:T(8,128)S(1)} custom-call(f32[11,32,32]{2,1,0:T(8,128)} %fusion.19), custom_call_target="Cholesky" | custom-call | tf_op jit(solution)/shard_map/jit(cholesky)/cholesky | solution.py:8
  220.4 0.1 compare_reduce_fusion
  220.5 0.1 select_bitcast_fusion
  220.6 27.1 %custom-call.8 = f32[11,1,32,32]{2,3,1,0:T(8,128)S(1)} custom-call(f32[11,1,32,32]{3,2,1,0:T(8,128)S(1)} %select_bitcast_fusion), custom_call_target="InvertDiagBlocksLowerTriangular" | custom-call | tf_op jit(solution)/shard_map/triangular_solve | solution.py:10
  247.7 0.5 fusion.17
  248.2 0.0 copy-done.13
  248.2 0.3 fusion.23
  248.5 0.9 fusion.30
  249.5 0.9 fusion.33
  250.4 0.0 copy-done
  250.4 0.0 copy-done.4
  250.4 0.6 convolution_bitcast_fusion.1
  251.0 0.4 fusion.6
  251.5 0.8 fusion.10
  252.3 1.1 pad_maximum_fusion
  253.4 0.0 copy-start.14
  253.4 0.0 copy-start.15
  253.4 0.0 copy-start.16
  253.4 0.0 all-reduce.5.cloned.1.call-update
  253.4 0.0 all-reduce.7.cloned.1.call-start
  253.5 105.9 %all-reduce.5.cloned.1.call-done = f32[11,32,768]{2,1,0:T(8,128)} async-done(((f32[11,32,768]{2,1,0:T(8,128)}), f32[11,32,768]{2,1,0:T(8,128)}) %all-reduce.5.cloned.1.call-update) | async-done | bytes 1081360 | tf_op jit(solution)/shard_map/psum | solution.py:73
  359.4 0.0 all-reduce.7.cloned.1.call-update
  359.4 0.0 copy-done.14
  359.4 0.0 copy-done.15
  359.4 0.0 copy-done.16
  359.4 0.6 multiply_subtract_fusion.3
  360.0 46.3 %all-reduce.7.cloned.1.call-done = f32[11,32,768]{2,1,0:T(8,128)} async-done(((f32[11,32,768]{2,1,0:T(8,128)}), f32[11,32,768]{2,1,0:T(8,128)}) %all-reduce.7.cloned.1.call-update) | async-done | bytes 1081360 | tf_op jit(solution)/shard_map/psum | solution.py:73
  406.3 0.0 copy-start.9
  406.3 1.4 broadcast_multiply_fusion
  407.7 0.0 copy-done.9
  407.7 0.1 copy-done.10
  407.8 2.0 fusion.50
  409.9 0.0 copy-done.11
  409.9 0.0 copy-done.12
  409.9 0.0 copy-start.8
  409.9 2.1 fusion.49
  412.0 0.0 copy-done.3
  412.0 0.0 copy-done.7
  412.0 0.0 copy-done.8
  412.0 2.5 fusion.48
  (11 shorter events, 0.1 us)
Async XLA Ops:
  7.2 4.1 copy-start.2
  7.2 4.1 copy-start.6
  7.2 51.0 %all-reduce.9.cloned.1.call-start = ((), (), s32[]{:S(2)}) async-start(), calls=%async_computation.2 | async-start | bytes 331776 | tf_op jit(solution)/shard_map/psum | solution.py:46
  8.6 4.9 %copy-start.1 = (f32[1,8,24,768]{3,2,1,0:T(8,128)S(1)}, f32[1,8,24,768]{3,2,1,0:T(8,128)}, u32[]{:S(2)}) copy-start(f32[1,8,24,768]{3,2,1,0:T(8,128)} %param.19) | copy-start | bytes 1769476
  8.6 4.9 %copy-start.5 = (bf16[1,8,24,768]{3,2,1,0:T(8,128)(2,1)S(1)}, bf16[1,8,24,768]{3,2,1,0:T(8,128)(2,1)}, u32[]{:S(2)}) copy-start(bf16[1,8,24,768]{3,2,1,0:T(8,128)(2,1)} %param.16) | copy-start | bytes 884740
  16.1 343.2 %all-reduce.5.cloned.1.call-start = ((), (), s32[]{:S(2)}) async-start(), calls=%async_computation | async-start | bytes 2162688 | tf_op jit(solution)/shard_map/psum | solution.py:73
  61.6 186.6 %copy-start.13 = (f32[8,32,24]{1,2,0:T(8,128)S(1)}, f32[8,32,24]{1,2,0:T(8,128)}, u32[]{:S(2)}) copy-start(f32[8,32,24]{1,2,0:T(8,128)} %get-tuple-element.17) | copy-start | bytes 73732
  186.7 63.7 %copy-start = (f32[1,256,768]{2,1,0:T(8,128)S(1)}, f32[1,256,768]{2,1,0:T(8,128)}, u32[]{:S(2)}) copy-start(f32[1,256,768]{2,1,0:T(8,128)} %param.21) | copy-start | bytes 2359300
  186.7 63.7 %copy-start.4 = (bf16[1,256,768]{2,1,0:T(8,128)(2,1)S(1)}, bf16[1,256,768]{2,1,0:T(8,128)(2,1)}, u32[]{:S(2)}) copy-start(bf16[1,256,768]{2,1,0:T(8,128)(2,1)} %param.18) | copy-start | bytes 1179652
  253.4 106.0 %copy-start.14 = (f32[3,24]{1,0:T(4,128)S(1)}, f32[3,24]{1,0:T(4,128)}, u32[]{:S(2)}) copy-start(f32[3,24]{1,0:T(4,128)} %param.29) | copy-start | bytes 868
  253.4 106.0 %copy-start.15 = (f32[3,24]{1,0:T(4,128)S(1)}, f32[3,24]{1,0:T(4,128)}, u32[]{:S(2)}) copy-start(f32[3,24]{1,0:T(4,128)} %param.30) | copy-start | bytes 868
  253.4 106.0 %copy-start.16 = (f32[3,24]{1,0:T(4,128)S(1)}, f32[3,24]{1,0:T(4,128)}, u32[]{:S(2)}) copy-start(f32[3,24]{1,0:T(4,128)} %get-tuple-element.18) | copy-start | bytes 868
  253.4 152.9 %all-reduce.7.cloned.1.call-start = ((), (), s32[]{:S(2)}) async-start(), calls=%async_computation.1 | async-start | bytes 2162688 | tf_op jit(solution)/shard_map/psum | solution.py:73
  406.3 1.4 copy-start.9
  406.3 1.6 copy-start.10
  407.8 4.2 copy-start.3
  407.8 2.1 copy-start.11
  407.8 2.1 copy-start.12
  409.9 2.1 copy-start.7
  409.9 2.1 copy-start.8
Sparse Core Ops, SparseCore 0:
  16.3 41.8 all-reduce.8
  253.5 105.7 all-reduce.4
  361.9 44.3 all-reduce.6
